TPU v7x, 32 devices: a whole 2x2x4 slice. The times are simulated.
32 devices in a mesh: tile: 8 (over z, y), clip: 4 (over x, core).
Axes of the slice: x: 2, y: 2, z: 4, core: 2. Of those that a mesh axis runs over, the one named last changes fastest.
Arguments:
- seq_rows: bfloat16 [32768, 512], P(('tile', 'clip'))
- plan_owner: int32 [32768], P(('tile', 'clip')), may hold values from 0 to 31, as said below
- plan_slot: int32 [32768], P(('tile', 'clip')), may hold values from 0 to 1023, as said below
- live_frames: int32 [4], replicated, may hold values from 1 to 4, as said below
- norm_gain: float32 [512], replicated, may hold values from 0.1 to 1.9
- norm_bias: float32 [512], replicated, may hold values from -3 to 3
- conv_weight: bfloat16 [3, 3, 512, 3, 256], replicated, may hold values from -0.0546875 to 0.0546875
- conv_bias: float32 [256], replicated, may hold values from -3 to 3
Outputs:
- decoded: bfloat16 [4, 8, 4, 8, 32, 256], P('clip', 'tile')
Inputs may be any that keep to these rules, and one draw needn't show every extreme that they name: `plan_owner`: owner o is tile o % 8 of clip o // 8. The 1024 rows of each device send 32 // 2 or 48 rows to each owner, so at most 48, which is reached. The pairs of plan_owner and plan_slot are all distinct: every slot of every owner receives exactly one row. `live_frames`: some clip has all 4 frames live.
All inputs are finite; a program needn't handle non-finite values.
Results may differ from a plain program's by a relative error of at most 0.004.
Values may be sent and summed in bfloat16 or wider, within the bound.
A program may use at most 128 MiB of HBM per device.

v0:
```python
import jax
import jax.numpy as jnp
from jax import lax
from jax.sharding import PartitionSpec as P

GROUPS = 32
LT = 4
TH = 8
TW = 32
GW = 4
EPSILON = 1e-06
HIGHEST = lax.Precision.HIGHEST


def shifted(block, axis, distance):
    devices = range(lax.axis_size(axis))
    route = [(i - distance, i) for i in devices if i - distance in devices]
    return lax.ppermute(block, axis, route)


def neighbour(values, offset):
    return shifted(values, "tile", offset)


def extend(tile_grid, column_tile, grid_cols):
    left_face = neighbour(tile_grid[:, :, -1:], 1)
    right_face = neighbour(tile_grid[:, :, :1], -1)
    left_face = jnp.where(column_tile > 0, left_face, jnp.zeros_like(left_face))
    right_face = jnp.where(column_tile < grid_cols - 1, right_face, jnp.zeros_like(right_face))
    widened = jnp.concatenate([left_face, tile_grid, right_face], axis=2)
    upper_face = neighbour(widened[:, -1:], grid_cols)
    lower_face = neighbour(widened[:, :1], -grid_cols)
    return jnp.concatenate([upper_face, widened, lower_face], axis=1)


def normalize(values, mean_channel, scale_channel, norm_gain, norm_bias):
    normed = (values.astype(jnp.float32) - mean_channel) * scale_channel * norm_gain + norm_bias
    return jax.nn.silu(normed)


def on_device(
    seq_rows, plan_owner, plan_slot, live_frames, norm_gain, norm_bias, conv_weight, conv_bias
):
    row_count, channels = seq_rows.shape
    out_width = conv_bias.shape[0]
    tile_count = lax.axis_size("tile")
    clip_count = lax.axis_size("clip")
    owner_count = tile_count * clip_count
    capacity = 3 * (row_count // owner_count) // 2
    per_group = channels // GROUPS
    plane_size = TH * TW
    voxel_total = float(plane_size * tile_count)
    row_index = jnp.arange(row_count, dtype=jnp.int32)
    owner_table = (plan_owner[:, None] == jnp.arange(owner_count, dtype=jnp.int32)[None, :]).astype(
        jnp.int32
    )
    ranking = jnp.sum((jnp.cumsum(owner_table, axis=0) - 1) * owner_table, axis=1)
    position = plan_owner * capacity + ranking
    my_clip = lax.axis_index("clip")
    my_tile = lax.axis_index("tile")
    frames_live = live_frames[my_clip]
    outgoing = (
        jnp.zeros((owner_count * capacity, channels), jnp.bfloat16).at[position].set(seq_rows)
    )
    slot_list = (
        jnp.full((owner_count * capacity,), row_count, jnp.int32).at[position].set(plan_slot)
    )
    outgoing = outgoing.reshape(clip_count, tile_count, capacity, channels)
    slot_list = slot_list.reshape(clip_count, tile_count, capacity)
    arrived, arrived_slots = (
        lax.all_to_all(
            lax.all_to_all(outgoing, "tile", split_axis=1, concat_axis=1, tiled=True),
            "clip",
            split_axis=0,
            concat_axis=0,
            tiled=True,
        ),
        lax.all_to_all(
            lax.all_to_all(slot_list, "tile", split_axis=1, concat_axis=1, tiled=True),
            "clip",
            split_axis=0,
            concat_axis=0,
            tiled=True,
        ),
    )
    tile_rows = (
        jnp.zeros((row_count, channels), jnp.bfloat16)
        .at[arrived_slots.reshape(-1)]
        .set(arrived.reshape(-1, channels), mode="drop")
    )
    grid_cols = GW
    grid_rows = tile_count // grid_cols
    column_tile = my_tile % grid_cols
    row_tile = my_tile // grid_cols
    live_frame = jnp.arange(LT) < frames_live
    values = tile_rows.astype(jnp.float32)
    live_row = (row_index // plane_size < frames_live).astype(jnp.float32)
    first_sum = jnp.dot(live_row, values, precision=HIGHEST).reshape(GROUPS, per_group).sum(axis=1)
    second_sum = (
        jnp.dot(live_row, values * values, precision=HIGHEST).reshape(GROUPS, per_group).sum(axis=1)
    )
    raw_padded = extend(tile_rows.reshape(LT, TH, TW, channels), column_tile, grid_cols)
    first_sum, second_sum = lax.psum((first_sum, second_sum), "tile")
    count_clip = per_group * frames_live.astype(jnp.float32) * voxel_total
    mean_group = first_sum / count_clip
    scale_group = lax.rsqrt(second_sum / count_clip - mean_group * mean_group + EPSILON)
    mean_channel = jnp.repeat(mean_group, per_group)
    scale_channel = jnp.repeat(scale_group, per_group)
    inside_rows = jnp.arange(TH + 2)
    inside_cols = jnp.arange(TW + 2)
    rows_inside = ((inside_rows > 0) | (row_tile > 0)) & (
        (inside_rows < TH + 1) | (row_tile < grid_rows - 1)
    )
    cols_inside = ((inside_cols > 0) | (column_tile > 0)) & (
        (inside_cols < TW + 1) | (column_tile < grid_cols - 1)
    )
    valid_mask = rows_inside[:, None] & cols_inside[None, :]
    activated = normalize(raw_padded, mean_channel, scale_channel, norm_gain, norm_bias)
    padded = jnp.where(valid_mask[None, :, :, None], activated, 0.0).astype(jnp.bfloat16)
    padded = jnp.concatenate(
        [jnp.zeros((2, TH + 2, TW + 2, channels), jnp.bfloat16), padded], axis=0
    )
    accumulated = jnp.zeros((LT, TH, TW, out_width), jnp.float32)
    for tap_t in range(3):
        for tap_h in range(3):
            slab_rows = padded[tap_t : tap_t + LT, tap_h : tap_h + TH].reshape(-1, channels)
            kernel = conv_weight[tap_t, tap_h].reshape(channels, 3 * out_width)
            product = jnp.dot(slab_rows, kernel, preferred_element_type=jnp.float32)
            product = product.reshape(LT, TH, TW + 2, 3, out_width)
            for tap_w in range(3):
                accumulated = accumulated + product[:, :, tap_w : tap_w + TW, tap_w]
    decoded = jnp.where(live_frame[:, None, None, None], accumulated + conv_bias, 0.0)
    return decoded.astype(jnp.bfloat16)[None, None]


def solution(mesh):
    return jax.shard_map(
        on_device,
        mesh=mesh,
        in_specs=(
            P(("tile", "clip"), None),
            P(("tile", "clip")),
            P(("tile", "clip")),
            P(),
            P(),
            P(),
            P(),
            P(),
        ),
        out_specs=P("clip", "tile", None, None, None, None),
        check_vma=False,
    )
```

profile of v0, /device:TPU:0, one launch (start us, length us, event | category | flops | bytes accessed | tf_op | source)
XLA Modules:
  0.0 185.9 jit_solution(9642833911319196824)
XLA Ops:
  0.7 9.0 %reduce-window.6 = s32[32,8,128]{2,1,0:T(8,128)S(1)} reduce-window(s32[32,8,128]{2,1,0:T(8,128)S(1)} %fusion.53, s32[]{:T(128)} %constant.69.clone.1), window={size=1x1x128 pad=0_0x0_0x127_0}, to_apply=%region_0.0 | reduce-window | flops 4161536 | bytes 262148 | tf_op jit(solution)/shard_map/reduce-window
  11.6 4.5 %scatter_custom_fusion = s32[1536]{0:T(1024)S(1)} fusion(s32[1024]{0:T(1024)S(1)} %compare_select_fusion.1, s32[1024]{0:T(1024)} %param.10, s32[]{:T(128)} %constant.80.clone.1), kind=kCustom, calls=%fused_computation.106 | custom fusion | bytes 6656 | tf_op jit(solution)/shard_map/scatter | solution.py:66
  16.9 7.3 %all-to-all-start = ((s32[8,1,192]{2,1,0:T(1,128)}), s32[8,1,192]{2,1,0:T(1,128)S(1)}, u32[]{:S(2)}, u32[]{:S(2)}) async-start(s32[8,1,192]{2,1,0:T(1,128)} %reshape.525), calls=%async_computation | async-start | bytes 16384 | tf_op jit(solution)/shard_map/all_to_all | solution.py:79
  24.1 6.0 %scatter_custom_fusion.1 = bf16[1536,512]{1,0:T(8,128)(2,1)S(1)} fusion(s32[1024]{0:T(1024)S(1)} %compare_select_fusion.1, bf16[1024,512]{1,0:T(8,128)(2,1)} %param.8, bf16[]{:T(256)} %constant.79.clone.1), kind=kCustom, calls=%fused_computation.80 | custom fusion | bytes 1573376 | tf_op jit(solution)/shard_map/scatter | solution.py:63
  31.5 6.0 %all-to-all-start.2 = ((bf16[4,8,48,512]{3,2,0,1:T(8,128)(2,1)}), bf16[4,8,48,512]{3,2,0,1:T(8,128)(2,1)S(1)}, u32[]{:S(2)}, u32[]{:S(2)}) async-start(bf16[4,8,48,512]{3,2,0,1:T(8,128)(2,1)} %copy.91), calls=%async_computation.2 | async-start | bytes 3145728 | tf_op jit(solution)/shard_map/all_to_all | solution.py:72
  39.4 34.5 %all-to-all-done.2 = bf16[4,8,48,512]{3,2,0,1:T(8,128)(2,1)S(1)} async-done(((bf16[4,8,48,512]{3,2,0,1:T(8,128)(2,1)}), bf16[4,8,48,512]{3,2,0,1:T(8,128)(2,1)S(1)}, u32[]{:S(2)}, u32[]{:S(2)}) %all-to-all-start.2) | async-done | bytes 1572896 | tf_op jit(solution)/shard_map/all_to_all | solution.py:72
  73.9 3.2 %all-to-all-start.1 = ((s32[4,1,384]{2,1,0:T(1,128)}), s32[4,1,384]{2,1,0:T(1,128)S(1)}, u32[]{:S(2)}, u32[]{:S(2)}) async-start(s32[4,1,384]{2,1,0:T(1,128)} %reshape.527), calls=%async_computation.1 | async-start | bytes 12288 | tf_op jit(solution)/shard_map/all_to_all | solution.py:78
  81.0 4.3 %all-to-all-start.3 = ((bf16[4,8,48,512]{3,2,1,0:T(8,128)(2,1)}), bf16[4,8,48,512]{3,2,1,0:T(8,128)(2,1)}, u32[]{:S(2)}, u32[]{:S(2)}) async-start(bf16[4,8,48,512]{3,2,1,0:T(8,128)(2,1)} %copy.92), calls=%async_computation.3 | async-start | bytes 3145728 | tf_op jit(solution)/shard_map/all_to_all | solution.py:71
  85.9 5.5 %fusion.67 = (bf16[1,1,512,3,256]{4,2,3,1,0:T(8,128)(2,1)}, bf16[1,1,512,3,256]{4,2,3,1,0:T(8,128)(2,1)}, bf16[1,1,512,3,256]{4,2,3,1,0:T(8,128)(2,1)}, bf16[1,1...) fusion(bf16[3,3,512,3,256]{4,2,3,1,0:T(8,128)(2,1)} %param.14), kind=kLoop, calls=%fused_computation.122 | loop fusion | bytes 14155776 | tf_op jit(solution)/shard_map/slice | solution.py:127
  92.8 2.4 %copy.138 = bf16[1,1,512,3,256]{2,4,3,1,0:T(8,128)(2,1)} copy(bf16[1,1,512,3,256]{4,2,3,1,0:T(8,128)(2,1)} %get-tuple-element.10) | data formatting | bytes 1572864
  95.1 2.3 %copy.137 = bf16[1,1,512,3,256]{2,4,3,1,0:T(8,128)(2,1)} copy(bf16[1,1,512,3,256]{4,2,3,1,0:T(8,128)(2,1)} %get-tuple-element.11) | data formatting | bytes 1572864
  97.4 2.3 %copy.135 = bf16[1,1,512,3,256]{2,4,3,1,0:T(8,128)(2,1)} copy(bf16[1,1,512,3,256]{4,2,3,1,0:T(8,128)(2,1)} %get-tuple-element.12) | data formatting | bytes 1572864
  104.6 2.3 %copy.131 = bf16[1,1,512,3,256]{2,4,3,1,0:T(8,128)(2,1)} copy(bf16[1,1,512,3,256]{4,2,3,1,0:T(8,128)(2,1)} %get-tuple-element.16) | data formatting | bytes 1572864
  109.7 8.0 %scatter_custom_fusion.2 = bf16[1024,512]{1,0:T(8,128)(2,1)S(1)} fusion(s32[1536]{0:T(1024)S(1)} %fusion.54, bf16[1536,512]{1,0:T(8,128)(2,1)} %bitcast.5, bf16[]{:T(256)} %constant.79.clone.1), kind=kCustom, calls=%fused_computation.82 | custom fusion | bytes 1049088 | tf_op jit(solution)/shard_map/scatter | solution.py:89
  118.7 3.3 %collective-permute-start = (bf16[4,8,1,512]{3,2,1,0:T(2,128)(2,1)S(1)}, bf16[4,8,1,512]{3,2,1,0:T(2,128)(2,1)S(1)}, u32[]{:S(2)}, u32[]{:S(2)}) collective-permute-start(bf16[4,8,1,512]{3,2,1,0:T(2,128)(2,1)S(1)} %get-tuple-element.20), channel_id=1, source_target_pairs={{0,4},{4,8},{8,12},{12,16},{16,20},{20,24},{24,28},{1,5},{5,9},{9,... | collective-permute-start | bytes 98312 | tf_op jit(solution)/shard_map/ppermute | solution.py:18
  124.0 20.7 %all-reduce.1 = (f32[32]{0:T(128)S(1)}, f32[32]{0:T(128)S(1)}) all-reduce(f32[32]{0:T(128)S(1)} %reduce_sum.28, f32[32]{0:T(128)S(1)} %reduce_sum.29), channel_id=1, replica_groups=mesh['tile'=8,'clip'=4] {'tile'}, use_global_device_ids=true, to_apply=%region_7.8 | all-reduce | flops 64 | bytes 512 | tf_op jit(solution)/shard_map/psum | solution.py:103
  149.1 6.4 %collective-permute-done.3 = bf16[4,1,34,512]{3,2,1,0:T(8,128)(2,1)S(1)} collective-permute-done((bf16[4,1,34,512]{3,2,1,0:T(8,128)(2,1)S(1)}, bf16[4,1,34,512]{3,2,1,0:T(8,128)(2,1)S(1)}, u32[]{:S(2)}, u32[]{:S(2)}) %collective-permute-start.3) | collective-permute-done | bytes 139296 | tf_op jit(solution)/shard_map/ppermute | solution.py:18
  155.5 2.5 %select_convert_fusion = bf16[4,10,34,512]{3,2,1,0:T(8,128)(2,1)S(1)} fusion(bf16[4,1,34,512]{3,2,1,0:T(8,128)(2,1)S(1)} %collective-permute-done.3, bf16[4,8,1,512]{3,2,1,0:T(2,128)(2,1)S(1)} %broadcast_select_fusion, bf16[4,8,32,512]{3,2,1,0:T(8,128)(2,1)S(1)} %bitcast.241, bf16[4,8,1,512]{3,2,1,0:T(2,128)(2,1)S(1)} %broadcast_select_fusion.1, ...), kind=kLoop, calls=%fused_computation.3 | loop fusion | flops 13926400 | bytes 2793812 | tf_op jit(solution)/shard_map/convert_element_type | solution.py:119
  158.0 2.5 %fusion.21 = f32[4,8,34,3,256]{4,2,1,0,3:T(8,128)S(1)} fusion(bf16[4,10,34,512]{3,2,1,0:T(8,128)(2,1)S(1)} %select_convert_fusion, bf16[1,1,512,3,256]{2,4,3,1,0:T(8,128)(2,1)} %copy.139), kind=kOutput, calls=%fused_computation.26 | convolution fusion | flops 855638016 | bytes 5439488 | tf_op jit(solution)/shard_map/dot_general | solution.py:128
  165.6 3.1 %fusion.19 = f32[4,8,34,3,256]{4,2,3,1,0:T(8,128)} fusion(bf16[4,10,34,512]{3,2,1,0:T(8,128)(2,1)S(1)} %select_convert_fusion, bf16[1,1,512,3,256]{2,4,3,1,0:T(8,128)(2,1)S(1)} %copy-done), kind=kOutput, calls=%fused_computation.24 | convolution fusion | flops 855638016 | bytes 5521408 | tf_op jit(solution)/shard_map/dot_general | solution.py:128
  168.7 3.2 %fusion.23 = f32[4,8,34,3,256]{4,2,1,0,3:T(8,128)} fusion(bf16[4,10,34,512]{3,2,1,0:T(8,128)(2,1)S(1)} %select_convert_fusion, bf16[1,1,512,3,256]{2,4,3,1,0:T(8,128)(2,1)S(1)} %copy-done.5), kind=kOutput, calls=%fused_computation.30 | convolution fusion | flops 855638016 | bytes 5439488 | tf_op jit(solution)/shard_map/dot_general | solution.py:128
  171.9 3.2 %fusion.22 = f32[4,8,34,3,256]{4,2,1,0,3:T(8,128)} fusion(bf16[4,10,34,512]{3,2,1,0:T(8,128)(2,1)S(1)} %select_convert_fusion, bf16[1,1,512,3,256]{2,4,3,1,0:T(8,128)(2,1)S(1)} %copy-done.4), kind=kOutput, calls=%fused_computation.28 | convolution fusion | flops 855638016 | bytes 5439488 | tf_op jit(solution)/shard_map/dot_general | solution.py:128
  175.1 3.2 %fusion.4 = f32[4,8,34,3,256]{4,2,3,1,0:T(8,128)} fusion(bf16[4,10,34,512]{3,2,1,0:T(8,128)(2,1)S(1)} %select_convert_fusion, bf16[1,1,512,3,256]{2,4,3,1,0:T(8,128)(2,1)S(1)} %copy.130), kind=kOutput, calls=%fused_computation.14 | convolution fusion | flops 855638016 | bytes 5521408 | tf_op jit(solution)/shard_map/dot_general | solution.py:128
  178.3 7.6 %fusion.27 = bf16[1,1,4,8,32,256]{5,4,3,2,1,0:T(8,128)(2,1)} fusion(f32[4,8,34,3,256]{4,2,1,0,3:T(8,128)S(1)} %fusion.21, f32[4,8,34,3,256]{4,2,1,0,3:T(8,128)} %fusion.22, f32[4,8,34,3,256]{4,2,1,0,3:T(8,128)} %fusion.23, f32[4,8,34,3,256]{4,2,3,1,0:T(8,128)} %fusion.19, f32[4,8,34,3,256]{4,2,3,1,0:T(8,128)S(1)} %fusion.16, ...), kind=kLoop, calls=%fused_computation.35 | loop fusion | flops 7602176 | bytes 28836868 | tf_op jit(solution)/shard_map/convert_element_type | solution.py:133
  (83 shorter events, 31.6 us)
Async XLA Ops:
  16.9 14.6 %all-to-all-start = ((s32[8,1,192]{2,1,0:T(1,128)}), s32[8,1,192]{2,1,0:T(1,128)S(1)}, u32[]{:S(2)}, u32[]{:S(2)}) async-start(s32[8,1,192]{2,1,0:T(1,128)} %reshape.525), calls=%async_computation | async-start | bytes 16384 | tf_op jit(solution)/shard_map/all_to_all | solution.py:79
  30.2 47.0 %copy-start.9 = (s32[4]{0:T(128)S(1)}, s32[4]{0:T(128)}, u32[]{:S(2)}) copy-start(s32[4]{0:T(128)} %param.11) | copy-start | bytes 52
  31.5 42.4 %all-to-all-start.2 = ((bf16[4,8,48,512]{3,2,0,1:T(8,128)(2,1)}), bf16[4,8,48,512]{3,2,0,1:T(8,128)(2,1)S(1)}, u32[]{:S(2)}, u32[]{:S(2)}) async-start(bf16[4,8,48,512]{3,2,0,1:T(8,128)(2,1)} %copy.91), calls=%async_computation.2 | async-start | bytes 3145728 | tf_op jit(solution)/shard_map/all_to_all | solution.py:72
  73.9 7.0 %all-to-all-start.1 = ((s32[4,1,384]{2,1,0:T(1,128)}), s32[4,1,384]{2,1,0:T(1,128)S(1)}, u32[]{:S(2)}, u32[]{:S(2)}) async-start(s32[4,1,384]{2,1,0:T(1,128)} %reshape.527), calls=%async_computation.1 | async-start | bytes 12288 | tf_op jit(solution)/shard_map/all_to_all | solution.py:78
  81.0 28.7 %all-to-all-start.3 = ((bf16[4,8,48,512]{3,2,1,0:T(8,128)(2,1)}), bf16[4,8,48,512]{3,2,1,0:T(8,128)(2,1)}, u32[]{:S(2)}, u32[]{:S(2)}) async-start(bf16[4,8,48,512]{3,2,1,0:T(8,128)(2,1)} %copy.92), calls=%async_computation.3 | async-start | bytes 3145728 | tf_op jit(solution)/shard_map/all_to_all | solution.py:71
  109.7 45.9 %copy-start.6 = (f32[512]{0:T(512)S(1)}, f32[512]{0:T(512)}, u32[]{:S(2)}) copy-start(f32[512]{0:T(512)} %param.13) | copy-start | bytes 6148
  109.7 45.9 %copy-start.7 = (f32[512]{0:T(512)S(1)}, f32[512]{0:T(512)}, u32[]{:S(2)}) copy-start(f32[512]{0:T(512)} %param.12) | copy-start | bytes 6148
  118.7 26.0 %collective-permute-start = (bf16[4,8,1,512]{3,2,1,0:T(2,128)(2,1)S(1)}, bf16[4,8,1,512]{3,2,1,0:T(2,128)(2,1)S(1)}, u32[]{:S(2)}, u32[]{:S(2)}) collective-permute-start(bf16[4,8,1,512]{3,2,1,0:T(2,128)(2,1)S(1)} %get-tuple-element.20), channel_id=1, source_target_pairs={{0,4},{4,8},{8,12},{12,16},{16,20},{20,24},{24,28},{1,5},{5,9},{9,... | collective-permute-start | bytes 98312 | tf_op jit(solution)/shard_map/ppermute | solution.py:18
  122.7 22.1 %collective-permute-start.1 = (bf16[4,8,1,512]{3,2,1,0:T(2,128)(2,1)S(1)}, bf16[4,8,1,512]{3,2,1,0:T(2,128)(2,1)S(1)}, u32[]{:S(2)}, u32[]{:S(2)}) collective-permute-start(bf16[4,8,1,512]{3,2,1,0:T(2,128)(2,1)S(1)} %get-tuple-element.21), channel_id=1, source_target_pairs={{4,0},{8,4},{12,8},{16,12},{20,16},{24,20},{28,24},{5,1},{9,5},{13... | collective-permute-start | bytes 98312 | tf_op jit(solution)/shard_map/ppermute | solution.py:18
  145.0 4.2 %collective-permute-start.2 = (bf16[4,1,34,512]{3,2,1,0:T(8,128)(2,1)S(1)}, bf16[4,1,34,512]{3,2,1,0:T(8,128)(2,1)S(1)}, u32[]{:S(2)}, u32[]{:S(2)}) collective-permute-start(bf16[4,1,34,512]{3,2,1,0:T(8,128)(2,1)S(1)} %get-tuple-element.18), channel_id=1, source_target_pairs={{0,16},{4,20},{8,24},{12,28},{1,17},{5,21},{9,25},{13,29},{2,18},{... | collective-permute-start | bytes 417800 | tf_op jit(solution)/shard_map/ppermute | solution.py:18
  146.3 9.2 %collective-permute-start.3 = (bf16[4,1,34,512]{3,2,1,0:T(8,128)(2,1)S(1)}, bf16[4,1,34,512]{3,2,1,0:T(8,128)(2,1)S(1)}, u32[]{:S(2)}, u32[]{:S(2)}) collective-permute-start(bf16[4,1,34,512]{3,2,1,0:T(8,128)(2,1)S(1)} %get-tuple-element.19), channel_id=1, source_target_pairs={{16,0},{20,4},{24,8},{28,12},{17,1},{21,5},{25,9},{29,13},{18,2},{... | collective-permute-start | bytes 417800 | tf_op jit(solution)/shard_map/ppermute | solution.py:18
  158.0 2.5 %copy-start.3 = (bf16[1,1,512,3,256]{2,4,3,1,0:T(8,128)(2,1)S(1)}, bf16[1,1,512,3,256]{2,4,3,1,0:T(8,128)(2,1)}, u32[]{:S(2)}) copy-start(bf16[1,1,512,3,256]{2,4,3,1,0:T(8,128)(2,1)} %copy.131) | copy-start | bytes 2359300
  160.5 1.3 copy-start.2
  163.0 1.3 copy-start.1
  164.3 1.3 copy-start
  165.6 3.2 %copy-start.5 = (bf16[1,1,512,3,256]{2,4,3,1,0:T(8,128)(2,1)S(1)}, bf16[1,1,512,3,256]{2,4,3,1,0:T(8,128)(2,1)}, u32[]{:S(2)}) copy-start(bf16[1,1,512,3,256]{2,4,3,1,0:T(8,128)(2,1)} %copy.137) | copy-start | bytes 2359300
  168.7 3.2 %copy-start.4 = (bf16[1,1,512,3,256]{2,4,3,1,0:T(8,128)(2,1)S(1)}, bf16[1,1,512,3,256]{2,4,3,1,0:T(8,128)(2,1)}, u32[]{:S(2)}) copy-start(bf16[1,1,512,3,256]{2,4,3,1,0:T(8,128)(2,1)} %copy.138) | copy-start | bytes 2359300
  175.1 3.2 %copy-start.8 = (f32[256]{0:T(256)S(1)}, f32[256]{0:T(256)}, u32[]{:S(2)}) copy-start(f32[256]{0:T(256)} %param.15) | copy-start | bytes 3076
where the time goes:
time: 187 us; the launch traced here: 186 us
  local copies, waits for them, and re-layouts  47 us (25%)
  waiting for transfers between devices  43.4 us (23%)
  starting transfers between devices  28.1 us (15%)
  other arithmetic  24.4 us (13%)
  matrix products  21.3 us (11%)
  blocking collectives  20.7 us (11%)
    all_to_all x1, waiting for transfers between devices, on_device(): lax.all_to_all(outgoing, 'tile', split_axis=1, concat_axis=1, tiled=True)  34.5 us
    psum x1, blocking collectives, on_device(): first_sum, second_sum = lax.psum((first_sum, second_sum), 'tile')  20.7 us
    dot_general x9, matrix products, on_device(): product = jnp.dot(slab_rows, kernel, preferred_element_type=jnp.float32)  20.2 us
    unnamed x33, local copies, waits for them, and re-layouts  18.3 us
    another operation x2, other arithmetic  9.04 us
    scatter x1, local copies, waits for them, and re-layouts, on_device(): tile_rows = jnp.zeros((row_count, channels), jnp.bfloat16).at[arrived_slo...  8 us
    ppermute x4, waiting for transfers between devices, shifted(): return lax.ppermute(block, axis, route)  7.63 us
    convert_element_type x1, other arithmetic, on_device(): return decoded.astype(jnp.bfloat16)[None, None]  7.58 us
  transfers between devices with their start and end apart: 8, of which 4 were waited for; matrix products, arithmetic and copies ran while one was open for 20% of the time, Pallas kernels for 0%

commit v1 on v0

--- a/solution.py
+++ b/solution.py
@@ -10,6 +10,22 @@
 GW = 4
 EPSILON = 1e-06
 HIGHEST = lax.Precision.HIGHEST
+
+
+def pairwise_exchange(array, axis, split, join):
+    ways, here = (lax.axis_size(axis), lax.axis_index(axis))
+    width = array.shape[split] // ways
+    shape = list(array.shape)
+    shape[split] = width
+    height = shape[join]
+    shape[join] = height * ways
+    full = jnp.zeros(shape, array.dtype)
+    for mask in range(ways):
+        part = lax.dynamic_slice_in_dim(array, (here ^ mask) * width, width, axis=split)
+        if mask:
+            part = lax.ppermute(part, axis, [(d, d ^ mask) for d in range(ways)])
+        full = lax.dynamic_update_slice_in_dim(full, part, (here ^ mask) * height, axis=join)
+    return full
 
 
 def shifted(block, axis, distance):
@@ -76,7 +92,7 @@
             tiled=True,
         ),
         lax.all_to_all(
-            lax.all_to_all(slot_list, "tile", split_axis=1, concat_axis=1, tiled=True),
+            pairwise_exchange(slot_list, "tile", 1, 1),
             "clip",
             split_axis=0,
             concat_axis=0,

time: 187 us -> 179 us (0.957)
  waiting for transfers between devices: 43.4 us -> 29.9 us
  starting transfers between devices: 28.1 us -> 33.7 us
    all_to_all x1, waiting for transfers between devices: 34.5 us -> 0.01 us  [on_device(): lax.all_to_all(outgoing, 'tile', split_axis=1, concat_axis=1, tiled=True)]
    ppermute x0 -> x7, waiting for transfers between devices: none -> 21.1 us  [pairwise_exchange(): part = lax.ppermute(part, axis, [(d, d ^ mask) for d in range(ways)])]
    ppermute x0 -> x7, starting transfers between devices: none -> 12.3 us  [pairwise_exchange(): part = lax.ppermute(part, axis, [(d, d ^ mask) for d in range(ways)])]
    all_to_all x2 -> x1, starting transfers between devices: 10.5 us -> 3.25 us  [on_device(): lax.all_to_all(pairwise_exchange(slot_list, 'tile', 1, 1), 'clip', split_...]
    unnamed x33 -> x31, local copies, waits for them, and re-layouts: 18.3 us -> 17.5 us
  transfers between devices with their start and end apart: 8 -> 14, of which waited for: 4 -> 6; matrix products, arithmetic and copies ran while one was open for 20% -> 19% of each run, Pallas kernels for 0% -> 0%
where the time goes in v1:
time: 179 us; the launch traced here: 178 us
  local copies, waits for them, and re-layouts  46.7 us (26%)
  starting transfers between devices  33.7 us (19%)
  waiting for transfers between devices  29.9 us (17%)
  other arithmetic  23.9 us (13%)
  matrix products  21.3 us (12%)
  blocking collectives  21.2 us (12%)
    psum x1, blocking collectives, on_device(): first_sum, second_sum = lax.psum((first_sum, second_sum), 'tile')  21.2 us
    ppermute x7, waiting for transfers between devices, pairwise_exchange(): part = lax.ppermute(part, axis, [(d, d ^ mask) for d in range(ways)])  21.1 us
    dot_general x9, matrix products, on_device(): product = jnp.dot(slab_rows, kernel, preferred_element_type=jnp.float32)  20.1 us
    unnamed x31, local copies, waits for them, and re-layouts  17.5 us
    ppermute x7, starting transfers between devices, pairwise_exchange(): part = lax.ppermute(part, axis, [(d, d ^ mask) for d in range(ways)])  12.3 us
    another operation x2, other arithmetic  9.04 us
    scatter x1, local copies, waits for them, and re-layouts, on_device(): tile_rows = jnp.zeros((row_count, channels), jnp.bfloat16).at[arrived_slo...  8.18 us
    ppermute x4, waiting for transfers between devices, shifted(): return lax.ppermute(block, axis, route)  7.63 us
  transfers between devices with their start and end apart: 14, of which 6 were waited for; matrix products, arithmetic and copies ran while one was open for 19% of the time, Pallas kernels for 0%

profile of v1, /device:TPU:0, one launch (start us, length us, event | category | flops | bytes accessed | tf_op | source)
XLA Modules:
  0.0 177.7 jit_solution(5816231173948608768)
XLA Ops:
  0.7 9.0 %reduce-window.6 = s32[32,8,128]{2,1,0:T(8,128)S(1)} reduce-window(s32[32,8,128]{2,1,0:T(8,128)S(1)} %fusion.53, s32[]{:T(128)} %constant.38.clone.1), window={size=1x1x128 pad=0_0x0_0x127_0}, to_apply=%region_0.0 | reduce-window | flops 4161536 | bytes 262148 | tf_op jit(solution)/shard_map/reduce-window
  11.6 6.0 %scatter_custom_fusion.1 = bf16[1536,512]{1,0:T(8,128)(2,1)S(1)} fusion(s32[1024]{0:T(1024)S(1)} %compare_select_fusion.1, bf16[1024,512]{1,0:T(8,128)(2,1)} %param.8, bf16[]{:T(256)} %constant.85.clone.1), kind=kCustom, calls=%fused_computation.80 | custom fusion | bytes 1573376 | tf_op jit(solution)/shard_map/scatter | solution.py:79
  19.0 7.4 %all-to-all-start.1 = ((bf16[4,8,48,512]{3,2,0,1:T(8,128)(2,1)}), bf16[4,8,48,512]{3,2,0,1:T(8,128)(2,1)S(1)}, u32[]{:S(2)}, u32[]{:S(2)}) async-start(bf16[4,8,48,512]{3,2,0,1:T(8,128)(2,1)} %copy.64), calls=%async_computation.1 | async-start | bytes 3145728 | tf_op jit(solution)/shard_map/all_to_all | solution.py:88
  26.4 4.5 %scatter_custom_fusion = s32[1536]{0:T(1024)S(1)} fusion(s32[1024]{0:T(1024)S(1)} %compare_select_fusion.1, s32[1024]{0:T(1024)} %param.10, s32[]{:T(128)} %constant.86.clone.1), kind=kCustom, calls=%fused_computation.106 | custom fusion | bytes 6656 | tf_op jit(solution)/shard_map/scatter | solution.py:82
  34.5 2.4 %collective-permute-start.4 = (s32[4,1,48]{2,1,0:T(1,128)S(1)}, s32[4,1,48]{2,1,0:T(1,128)S(1)}, u32[]{:S(2)}, u32[]{:S(2)}) collective-permute-start(s32[4,1,48]{2,1,0:T(1,128)S(1)} %get-tuple-element.24), channel_id=1, source_target_pairs={{0,20},{4,16},{8,28},{12,24},{16,4},{20,0},{24,12},{28,8},{1,21},{... | collective-permute-start | bytes 2312 | tf_op jit(solution)/shard_map/ppermute | solution.py:26
  38.9 13.9 %collective-permute-done.1 = s32[4,1,48]{2,1,0:T(1,128)S(1)} collective-permute-done((s32[4,1,48]{2,1,0:T(1,128)S(1)}, s32[4,1,48]{2,1,0:T(1,128)S(1)}, u32[]{:S(2)}, u32[]{:S(2)}) %collective-permute-start.1) | collective-permute-done | bytes 800 | tf_op jit(solution)/shard_map/ppermute | solution.py:26
  52.8 2.9 %collective-permute-start.5 = (s32[4,1,48]{2,1,0:T(1,128)S(1)}, s32[4,1,48]{2,1,0:T(1,128)S(1)}, u32[]{:S(2)}, u32[]{:S(2)}) collective-permute-start(s32[4,1,48]{2,1,0:T(1,128)S(1)} %get-tuple-element.23), channel_id=1, source_target_pairs={{0,24},{4,28},{8,16},{12,20},{16,8},{20,12},{24,0},{28,4},{1,25},{... | collective-permute-start | bytes 2312 | tf_op jit(solution)/shard_map/ppermute | solution.py:26
  57.3 6.4 %collective-permute-done.3 = s32[4,1,48]{2,1,0:T(1,128)S(1)} collective-permute-done((s32[4,1,48]{2,1,0:T(1,128)S(1)}, s32[4,1,48]{2,1,0:T(1,128)S(1)}, u32[]{:S(2)}, u32[]{:S(2)}) %collective-permute-start.3) | collective-permute-done | bytes 800 | tf_op jit(solution)/shard_map/ppermute | solution.py:26
  65.3 3.2 %all-to-all-start = ((s32[4,1,384]{2,1,0:T(1,128)}), s32[4,1,384]{2,1,0:T(1,128)S(1)}, u32[]{:S(2)}, u32[]{:S(2)}) async-start(s32[4,1,384]{2,1,0:T(1,128)} %reshape.525), calls=%async_computation | async-start | bytes 12288 | tf_op jit(solution)/shard_map/all_to_all | solution.py:94
  72.3 4.3 %all-to-all-start.2 = ((bf16[4,8,48,512]{3,2,1,0:T(8,128)(2,1)}), bf16[4,8,48,512]{3,2,1,0:T(8,128)(2,1)}, u32[]{:S(2)}, u32[]{:S(2)}) async-start(bf16[4,8,48,512]{3,2,1,0:T(8,128)(2,1)} %copy.65), calls=%async_computation.2 | async-start | bytes 3145728 | tf_op jit(solution)/shard_map/all_to_all | solution.py:87
  77.4 5.4 %fusion.67 = (bf16[1,1,512,3,256]{4,2,3,1,0:T(8,128)(2,1)}, bf16[1,1,512,3,256]{4,2,3,1,0:T(8,128)(2,1)}, bf16[1,1,512,3,256]{4,2,3,1,0:T(8,128)(2,1)}, bf16[1,1...) fusion(bf16[3,3,512,3,256]{4,2,3,1,0:T(8,128)(2,1)} %param.14), kind=kLoop, calls=%fused_computation.130 | loop fusion | bytes 14155776 | tf_op jit(solution)/shard_map/slice | solution.py:143
  84.2 2.4 %copy.111 = bf16[1,1,512,3,256]{2,4,3,1,0:T(8,128)(2,1)} copy(bf16[1,1,512,3,256]{4,2,3,1,0:T(8,128)(2,1)} %get-tuple-element.10) | data formatting | bytes 1572864
  86.6 2.3 %copy.110 = bf16[1,1,512,3,256]{2,4,3,1,0:T(8,128)(2,1)} copy(bf16[1,1,512,3,256]{4,2,3,1,0:T(8,128)(2,1)} %get-tuple-element.11) | data formatting | bytes 1572864
  101.7 8.2 %scatter_custom_fusion.2 = bf16[1024,512]{1,0:T(8,128)(2,1)S(1)} fusion(s32[1536]{0:T(1024)S(1)} %fusion.54, bf16[1536,512]{1,0:T(8,128)(2,1)} %bitcast.5, bf16[]{:T(256)} %constant.85.clone.1), kind=kCustom, calls=%fused_computation.82 | custom fusion | bytes 1049088 | tf_op jit(solution)/shard_map/scatter | solution.py:105
  110.9 2.5 %collective-permute-start.7 = (bf16[4,8,1,512]{3,2,1,0:T(2,128)(2,1)S(1)}, bf16[4,8,1,512]{3,2,1,0:T(2,128)(2,1)S(1)}, u32[]{:S(2)}, u32[]{:S(2)}) collective-permute-start(bf16[4,8,1,512]{3,2,1,0:T(2,128)(2,1)S(1)} %get-tuple-element.20), channel_id=1, source_target_pairs={{0,4},{4,8},{8,12},{12,16},{16,20},{20,24},{24,28},{1,5},{5,9},{9,... | collective-permute-start | bytes 98312 | tf_op jit(solution)/shard_map/ppermute | solution.py:34
  115.4 21.2 %all-reduce.1 = (f32[32]{0:T(128)S(1)}, f32[32]{0:T(128)S(1)}) all-reduce(f32[32]{0:T(128)S(1)} %reduce_sum.28, f32[32]{0:T(128)S(1)} %reduce_sum.29), channel_id=1, replica_groups=mesh['tile'=8,'clip'=4] {'tile'}, use_global_device_ids=true, to_apply=%region_7.8 | all-reduce | flops 64 | bytes 512 | tf_op jit(solution)/shard_map/psum | solution.py:119
  141.0 6.4 %collective-permute-done.10 = bf16[4,1,34,512]{3,2,1,0:T(8,128)(2,1)S(1)} collective-permute-done((bf16[4,1,34,512]{3,2,1,0:T(8,128)(2,1)S(1)}, bf16[4,1,34,512]{3,2,1,0:T(8,128)(2,1)S(1)}, u32[]{:S(2)}, u32[]{:S(2)}) %collective-permute-start.10) | collective-permute-done | bytes 139296 | tf_op jit(solution)/shard_map/ppermute | solution.py:34
  147.4 2.5 %select_convert_fusion = bf16[4,10,34,512]{3,2,1,0:T(8,128)(2,1)S(1)} fusion(bf16[4,1,34,512]{3,2,1,0:T(8,128)(2,1)S(1)} %collective-permute-done.10, bf16[4,8,1,512]{3,2,1,0:T(2,128)(2,1)S(1)} %broadcast_select_fusion, bf16[4,8,32,512]{3,2,1,0:T(8,128)(2,1)S(1)} %bitcast.237, bf16[4,8,1,512]{3,2,1,0:T(2,128)(2,1)S(1)} %broadcast_select_fusion.1, ...), kind=kLoop, calls=%fused_computation.3 | loop fusion | flops 13926400 | bytes 2793812 | tf_op jit(solution)/shard_map/convert_element_type | solution.py:135
  149.9 2.5 %fusion.21 = f32[4,8,34,3,256]{4,2,1,0,3:T(8,128)S(1)} fusion(bf16[4,10,34,512]{3,2,1,0:T(8,128)(2,1)S(1)} %select_convert_fusion, bf16[1,1,512,3,256]{2,4,3,1,0:T(8,128)(2,1)} %copy.112), kind=kOutput, calls=%fused_computation.26 | convolution fusion | flops 855638016 | bytes 5439488 | tf_op jit(solution)/shard_map/dot_general | solution.py:144
  157.5 3.1 %fusion.19 = f32[4,8,34,3,256]{4,2,3,1,0:T(8,128)} fusion(bf16[4,10,34,512]{3,2,1,0:T(8,128)(2,1)S(1)} %select_convert_fusion, bf16[1,1,512,3,256]{2,4,3,1,0:T(8,128)(2,1)S(1)} %copy-done), kind=kOutput, calls=%fused_computation.24 | convolution fusion | flops 855638016 | bytes 5521408 | tf_op jit(solution)/shard_map/dot_general | solution.py:144
  160.6 3.1 %fusion.23 = f32[4,8,34,3,256]{4,2,1,0,3:T(8,128)} fusion(bf16[4,10,34,512]{3,2,1,0:T(8,128)(2,1)S(1)} %select_convert_fusion, bf16[1,1,512,3,256]{2,4,3,1,0:T(8,128)(2,1)S(1)} %copy-done.5), kind=kOutput, calls=%fused_computation.30 | convolution fusion | flops 855638016 | bytes 5439488 | tf_op jit(solution)/shard_map/dot_general | solution.py:144
  163.7 3.2 %fusion.22 = f32[4,8,34,3,256]{4,2,1,0,3:T(8,128)} fusion(bf16[4,10,34,512]{3,2,1,0:T(8,128)(2,1)S(1)} %select_convert_fusion, bf16[1,1,512,3,256]{2,4,3,1,0:T(8,128)(2,1)S(1)} %copy-done.4), kind=kOutput, calls=%fused_computation.28 | convolution fusion | flops 855638016 | bytes 5439488 | tf_op jit(solution)/shard_map/dot_general | solution.py:144
  167.0 3.2 %fusion.4 = f32[4,8,34,3,256]{4,2,3,1,0:T(8,128)} fusion(bf16[4,10,34,512]{3,2,1,0:T(8,128)(2,1)S(1)} %select_convert_fusion, bf16[1,1,512,3,256]{2,4,3,1,0:T(8,128)(2,1)S(1)} %copy.103), kind=kOutput, calls=%fused_computation.14 | convolution fusion | flops 855638016 | bytes 5521408 | tf_op jit(solution)/shard_map/dot_general | solution.py:144
  170.2 7.6 %fusion.27 = bf16[1,1,4,8,32,256]{5,4,3,2,1,0:T(8,128)(2,1)} fusion(f32[4,8,34,3,256]{4,2,1,0,3:T(8,128)S(1)} %fusion.21, f32[4,8,34,3,256]{4,2,1,0,3:T(8,128)} %fusion.22, f32[4,8,34,3,256]{4,2,1,0,3:T(8,128)} %fusion.23, f32[4,8,34,3,256]{4,2,3,1,0:T(8,128)} %fusion.19, f32[4,8,34,3,256]{4,2,3,1,0:T(8,128)S(1)} %fusion.16, ...), kind=kLoop, calls=%fused_computation.35 | loop fusion | flops 7602176 | bytes 28836868 | tf_op jit(solution)/shard_map/convert_element_type | solution.py:149
  (100 shorter events, 43.0 us)
Async XLA Ops:
  19.0 49.7 %copy-start.9 = (s32[4]{0:T(128)S(1)}, s32[4]{0:T(128)}, u32[]{:S(2)}) copy-start(s32[4]{0:T(128)} %param.11) | copy-start | bytes 52
  19.0 46.4 %all-to-all-start.1 = ((bf16[4,8,48,512]{3,2,0,1:T(8,128)(2,1)}), bf16[4,8,48,512]{3,2,0,1:T(8,128)(2,1)S(1)}, u32[]{:S(2)}, u32[]{:S(2)}) async-start(bf16[4,8,48,512]{3,2,0,1:T(8,128)(2,1)} %copy.64), calls=%async_computation.1 | async-start | bytes 3145728 | tf_op jit(solution)/shard_map/all_to_all | solution.py:88
  31.0 21.8 %collective-permute-start.1 = (s32[4,1,48]{2,1,0:T(1,128)S(1)}, s32[4,1,48]{2,1,0:T(1,128)S(1)}, u32[]{:S(2)}, u32[]{:S(2)}) collective-permute-start(s32[4,1,48]{2,1,0:T(1,128)S(1)} %get-tuple-element.27), channel_id=1, source_target_pairs={{0,8},{4,12},{8,0},{12,4},{16,24},{20,28},{24,16},{28,20},{1,9},{5... | collective-permute-start | bytes 2312 | tf_op jit(solution)/shard_map/ppermute | solution.py:26
  33.0 22.6 %collective-permute-start = (s32[4,1,48]{2,1,0:T(1,128)S(1)}, s32[4,1,48]{2,1,0:T(1,128)S(1)}, u32[]{:S(2)}, u32[]{:S(2)}) collective-permute-start(s32[4,1,48]{2,1,0:T(1,128)S(1)} %get-tuple-element.28), channel_id=1, source_target_pairs={{0,4},{4,0},{8,12},{12,8},{16,20},{20,16},{24,28},{28,24},{1,5},{5... | collective-permute-start | bytes 2312 | tf_op jit(solution)/shard_map/ppermute | solution.py:26
  34.5 30.0 %collective-permute-start.4 = (s32[4,1,48]{2,1,0:T(1,128)S(1)}, s32[4,1,48]{2,1,0:T(1,128)S(1)}, u32[]{:S(2)}, u32[]{:S(2)}) collective-permute-start(s32[4,1,48]{2,1,0:T(1,128)S(1)} %get-tuple-element.24), channel_id=1, source_target_pairs={{0,20},{4,16},{8,28},{12,24},{16,4},{20,0},{24,12},{28,8},{1,21},{... | collective-permute-start | bytes 2312 | tf_op jit(solution)/shard_map/ppermute | solution.py:26
  36.9 20.4 %collective-permute-start.2 = (s32[4,1,48]{2,1,0:T(1,128)S(1)}, s32[4,1,48]{2,1,0:T(1,128)S(1)}, u32[]{:S(2)}, u32[]{:S(2)}) collective-permute-start(s32[4,1,48]{2,1,0:T(1,128)S(1)} %get-tuple-element.26), channel_id=1, source_target_pairs={{0,12},{4,8},{8,4},{12,0},{16,28},{20,24},{24,20},{28,16},{1,13},{... | collective-permute-start | bytes 2312 | tf_op jit(solution)/shard_map/ppermute | solution.py:26
  38.3 25.3 %collective-permute-start.3 = (s32[4,1,48]{2,1,0:T(1,128)S(1)}, s32[4,1,48]{2,1,0:T(1,128)S(1)}, u32[]{:S(2)}, u32[]{:S(2)}) collective-permute-start(s32[4,1,48]{2,1,0:T(1,128)S(1)} %get-tuple-element.25), channel_id=1, source_target_pairs={{0,16},{4,20},{8,24},{12,28},{16,0},{20,4},{24,8},{28,12},{1,17},{... | collective-permute-start | bytes 2312 | tf_op jit(solution)/shard_map/ppermute | solution.py:26
  52.8 11.8 %collective-permute-start.5 = (s32[4,1,48]{2,1,0:T(1,128)S(1)}, s32[4,1,48]{2,1,0:T(1,128)S(1)}, u32[]{:S(2)}, u32[]{:S(2)}) collective-permute-start(s32[4,1,48]{2,1,0:T(1,128)S(1)} %get-tuple-element.23), channel_id=1, source_target_pairs={{0,24},{4,28},{8,16},{12,20},{16,8},{20,12},{24,0},{28,4},{1,25},{... | collective-permute-start | bytes 2312 | tf_op jit(solution)/shard_map/ppermute | solution.py:26
  55.7 8.9 %collective-permute-start.6 = (s32[4,1,48]{2,1,0:T(1,128)S(1)}, s32[4,1,48]{2,1,0:T(1,128)S(1)}, u32[]{:S(2)}, u32[]{:S(2)}) collective-permute-start(s32[4,1,48]{2,1,0:T(1,128)S(1)} %get-tuple-element.22), channel_id=1, source_target_pairs={{0,28},{4,24},{8,20},{12,16},{16,12},{20,8},{24,4},{28,0},{1,29},{... | collective-permute-start | bytes 2312 | tf_op jit(solution)/shard_map/ppermute | solution.py:26
  65.3 7.0 %all-to-all-start = ((s32[4,1,384]{2,1,0:T(1,128)}), s32[4,1,384]{2,1,0:T(1,128)S(1)}, u32[]{:S(2)}, u32[]{:S(2)}) async-start(s32[4,1,384]{2,1,0:T(1,128)} %reshape.525), calls=%async_computation | async-start | bytes 12288 | tf_op jit(solution)/shard_map/all_to_all | solution.py:94
  72.3 29.3 %all-to-all-start.2 = ((bf16[4,8,48,512]{3,2,1,0:T(8,128)(2,1)}), bf16[4,8,48,512]{3,2,1,0:T(8,128)(2,1)}, u32[]{:S(2)}, u32[]{:S(2)}) async-start(bf16[4,8,48,512]{3,2,1,0:T(8,128)(2,1)} %copy.65), calls=%async_computation.2 | async-start | bytes 3145728 | tf_op jit(solution)/shard_map/all_to_all | solution.py:87
  101.6 45.8 %copy-start.6 = (f32[512]{0:T(512)S(1)}, f32[512]{0:T(512)}, u32[]{:S(2)}) copy-start(f32[512]{0:T(512)} %param.13) | copy-start | bytes 6148
  101.7 45.8 %copy-start.7 = (f32[512]{0:T(512)S(1)}, f32[512]{0:T(512)}, u32[]{:S(2)}) copy-start(f32[512]{0:T(512)} %param.12) | copy-start | bytes 6148
  110.9 25.7 %collective-permute-start.7 = (bf16[4,8,1,512]{3,2,1,0:T(2,128)(2,1)S(1)}, bf16[4,8,1,512]{3,2,1,0:T(2,128)(2,1)S(1)}, u32[]{:S(2)}, u32[]{:S(2)}) collective-permute-start(bf16[4,8,1,512]{3,2,1,0:T(2,128)(2,1)S(1)} %get-tuple-element.20), channel_id=1, source_target_pairs={{0,4},{4,8},{8,12},{12,16},{16,20},{20,24},{24,28},{1,5},{5,9},{9,... | collective-permute-start | bytes 98312 | tf_op jit(solution)/shard_map/ppermute | solution.py:34
  114.1 22.6 %collective-permute-start.8 = (bf16[4,8,1,512]{3,2,1,0:T(2,128)(2,1)S(1)}, bf16[4,8,1,512]{3,2,1,0:T(2,128)(2,1)S(1)}, u32[]{:S(2)}, u32[]{:S(2)}) collective-permute-start(bf16[4,8,1,512]{3,2,1,0:T(2,128)(2,1)S(1)} %get-tuple-element.21), channel_id=1, source_target_pairs={{4,0},{8,4},{12,8},{16,12},{20,16},{24,20},{28,24},{5,1},{9,5},{13... | collective-permute-start | bytes 98312 | tf_op jit(solution)/shard_map/ppermute | solution.py:34
  136.8 4.2 %collective-permute-start.9 = (bf16[4,1,34,512]{3,2,1,0:T(8,128)(2,1)S(1)}, bf16[4,1,34,512]{3,2,1,0:T(8,128)(2,1)S(1)}, u32[]{:S(2)}, u32[]{:S(2)}) collective-permute-start(bf16[4,1,34,512]{3,2,1,0:T(8,128)(2,1)S(1)} %get-tuple-element.18), channel_id=1, source_target_pairs={{0,16},{4,20},{8,24},{12,28},{1,17},{5,21},{9,25},{13,29},{2,18},{... | collective-permute-start | bytes 417800 | tf_op jit(solution)/shard_map/ppermute | solution.py:34
  138.2 9.2 %collective-permute-start.10 = (bf16[4,1,34,512]{3,2,1,0:T(8,128)(2,1)S(1)}, bf16[4,1,34,512]{3,2,1,0:T(8,128)(2,1)S(1)}, u32[]{:S(2)}, u32[]{:S(2)}) collective-permute-start(bf16[4,1,34,512]{3,2,1,0:T(8,128)(2,1)S(1)} %get-tuple-element.19), channel_id=1, source_target_pairs={{16,0},{20,4},{24,8},{28,12},{17,1},{21,5},{25,9},{29,13},{18,2},{... | collective-permute-start | bytes 417800 | tf_op jit(solution)/shard_map/ppermute | solution.py:34
  149.9 2.5 %copy-start.3 = (bf16[1,1,512,3,256]{2,4,3,1,0:T(8,128)(2,1)S(1)}, bf16[1,1,512,3,256]{2,4,3,1,0:T(8,128)(2,1)}, u32[]{:S(2)}) copy-start(bf16[1,1,512,3,256]{2,4,3,1,0:T(8,128)(2,1)} %copy.104) | copy-start | bytes 2359300
  152.4 1.3 copy-start.2
  154.9 1.3 copy-start.1
  156.2 1.3 copy-start
  157.4 3.1 %copy-start.5 = (bf16[1,1,512,3,256]{2,4,3,1,0:T(8,128)(2,1)S(1)}, bf16[1,1,512,3,256]{2,4,3,1,0:T(8,128)(2,1)}, u32[]{:S(2)}) copy-start(bf16[1,1,512,3,256]{2,4,3,1,0:T(8,128)(2,1)} %copy.110) | copy-start | bytes 2359300
  160.6 3.1 %copy-start.4 = (bf16[1,1,512,3,256]{2,4,3,1,0:T(8,128)(2,1)S(1)}, bf16[1,1,512,3,256]{2,4,3,1,0:T(8,128)(2,1)}, u32[]{:S(2)}) copy-start(bf16[1,1,512,3,256]{2,4,3,1,0:T(8,128)(2,1)} %copy.111) | copy-start | bytes 2359300
  167.0 3.2 %copy-start.8 = (f32[256]{0:T(256)S(1)}, f32[256]{0:T(256)}, u32[]{:S(2)}) copy-start(f32[256]{0:T(256)} %param.15) | copy-start | bytes 3076
